TPU v7x, 128 devices: a whole 4x4x4 slice. The times are simulated.
128 devices in a mesh: lon: 16 (over x_hi, z, core), lat: 8 (over y, x_lo).
Axes of the slice: x: 4 (x_hi: 2, x_lo: 2; x = x_hi * 2 + x_lo), y: 4, z: 4, core: 2. Of those that a mesh axis runs over, the one named last changes fastest.
Arguments:
- state: float32 [150, 256, 2048], P(None, 'lat', 'lon'), may hold values from -6 to 6
- diffusivity: float32 [150, 256, 2048], P(None, 'lat', 'lon'), may hold values from 0.02 to 0.24
- sea_mask: int32 [75, 256, 2048], P(None, 'lat', 'lon'), may hold values 0 or 1
- send_cols: int32 [128, 3072], P(('lon', 'lat')), may hold values from 0 to 4096, as said below
- obs_slots: int32 [4, 262144], P(None, ('lon', 'lat')), may hold values from 0 to 3071, as said below
- obs_weights: float32 [4, 262144], P(None, ('lon', 'lat')), may hold values from 0.05 to 0.5
- obs_precision: float32 [150, 262144], P(None, ('lon', 'lat')), may hold values from 0.25 to 4
Outputs:
- product: float32 [150, 256, 2048], P(None, 'lat', 'lon')
- equivalents: float32 [150, 262144], P(None, ('lon', 'lat'))
Inputs may be any that keep to these rules, and one draw needn't show every extreme that they name: `send_cols`: for each device s and owner o the first n entries of the owner's 24 entries are local column indices below 4096, the rest are 4096; n is at least 1 and at most 24; every device has some owner with n = 24, and some owner receives 24 columns from every device. `obs_slots`: every slot named refers to a live entry: for owner o, slot s * 24 + p with p below the number of live entries of device s for owner o.
All inputs are finite; a program needn't handle non-finite values. No bound on the sum of `sea_mask` on one device may be relied on, other than what follows from the above.
Results may differ from a plain program's by a relative error of at most 0.00002.
Values sent between devices are 32-bit elements; how exact they have to be, the bound alone decides.
A program may use at most 128 MiB of HBM per device.

v0:
```python
import jax
import jax.numpy as jnp
from jax import lax
from jax.sharding import PartitionSpec as P

SWEEPS = 2


def with_halo(cells, sides, width, closed):
    for axis, dim in sides:
        count = lax.axis_size(axis)
        ends = count if closed else count - 1
        head = lax.slice_in_dim(cells, 0, width, axis=dim)
        tail = lax.slice_in_dim(cells, cells.shape[dim] - width, cells.shape[dim], axis=dim)
        cells = jnp.concatenate(
            [
                lax.ppermute(tail, axis, [(i, (i + 1) % count) for i in range(ends)]),
                cells,
                lax.ppermute(head, axis, [((i + 1) % count, i) for i in range(ends)]),
            ],
            axis=dim,
        )
    return cells


def trimmed(array, margin):
    return array[:, margin : array.shape[1] - margin, margin : array.shape[2] - margin]


def relax_step(wide_field, wide_coef):
    centre = wide_field[:, 1:-1, 1:-1]
    centre_coef = wide_coef[:, 1:-1, 1:-1]
    total = jnp.minimum(centre_coef, wide_coef[:, 2:, 1:-1]) * (wide_field[:, 2:, 1:-1] - centre)
    total = total + jnp.minimum(centre_coef, wide_coef[:, :-2, 1:-1]) * (
        wide_field[:, :-2, 1:-1] - centre
    )
    total = total + jnp.minimum(centre_coef, wide_coef[:, 1:-1, :-2]) * (
        wide_field[:, 1:-1, :-2] - centre
    )
    total = total + jnp.minimum(centre_coef, wide_coef[:, 1:-1, 2:]) * (
        wide_field[:, 1:-1, 2:] - centre
    )
    return centre + total


def coefficient_rims(conduct):
    along_lon = with_halo(conduct, (("lon", 2),), SWEEPS, True)
    return with_halo(along_lon, (("lat", 1),), SWEEPS, False)


def single_rims(field):
    along_lon = with_halo(field, (("lon", 2),), 1, True)
    return with_halo(along_lon, (("lat", 1),), 1, False)


def diffuse(field, wide_coef):
    inner_coef = trimmed(wide_coef, SWEEPS - 1)
    for sweep in range(SWEEPS):
        field = relax_step(single_rims(field), inner_coef)
    return field


def to_owners(outgoing):
    return lax.all_to_all(outgoing, ("lon", "lat"), split_axis=1, concat_axis=1, tiled=True)


def to_sources(returned):
    return lax.all_to_all(returned, ("lon", "lat"), split_axis=1, concat_axis=1, tiled=True)


def on_device(state, diffusivity, sea_mask, send_cols, obs_slots, obs_weights, obs_precision):
    vals = state.shape[0]
    cell_count = state.shape[1] * state.shape[2]
    sea_float = sea_mask.astype(jnp.float32)
    conduct = diffusivity * jnp.concatenate([sea_float, sea_float], axis=0)
    wide_coef = coefficient_rims(conduct)
    smooth = diffuse(state, wide_coef)
    flat_cols = jnp.concatenate(
        [smooth.reshape(vals, cell_count), jnp.zeros((vals, 1), jnp.float32)], axis=1
    )
    send_index = send_cols[0]
    outgoing = jnp.take(flat_cols, send_index, axis=1)
    received = to_owners(outgoing)
    slot_count = outgoing.shape[1]
    taps, obs_count = obs_slots.shape
    all_slots = obs_slots.reshape(taps * obs_count)
    picked = jnp.take(received, all_slots, axis=1).reshape(vals, taps, obs_count)
    equivalents = jnp.sum(picked * obs_weights[None, :, :], axis=1)
    weighted = obs_precision * equivalents
    spread = (weighted[:, None, :] * obs_weights[None, :, :]).reshape(vals, taps * obs_count)
    returned = jnp.zeros((vals, slot_count), jnp.float32).at[:, all_slots].add(spread)
    incoming = to_sources(returned)
    adjoint_cols = jnp.zeros((vals, cell_count + 1), jnp.float32).at[:, send_index].add(incoming)
    adjoint_field = adjoint_cols[:, :cell_count].reshape(state.shape)
    product = state + diffuse(adjoint_field, wide_coef)
    return (product, equivalents)


def solution(mesh):
    placed = (
        P(None, "lat", "lon"),
        P(None, "lat", "lon"),
        P(None, "lat", "lon"),
        P(("lon", "lat"), None),
        P(None, ("lon", "lat")),
        P(None, ("lon", "lat")),
        P(None, ("lon", "lat")),
    )
    return jax.shard_map(
        on_device,
        mesh=mesh,
        in_specs=placed,
        out_specs=(P(None, "lat", "lon"), P(None, ("lon", "lat"))),
        check_vma=False,
    )
```

profile of v0, /device:TPU:8, one launch (start us, length us, event | category | flops | bytes accessed | tf_op | source)
XLA Modules:
  0.0 480.9 jit_solution(6703903125890023950)
XLA Ops:
  0.6 4.7 fusion.66
  10.9 6.0 %collective-permute-start.4 = (f32[150,32,1]{0,1,2:T(8,128)S(1)}, f32[150,32,1]{0,1,2:T(8,128)S(1)}, u32[]{:S(2)}, u32[]{:S(2)}) collective-permute-start(f32[150,32,1]{0,1,2:T(8,128)S(1)} %copy.137), channel_id=1, source_target_pairs={{8,0},{16,8},{24,16},{32,24},{40,32},{48,40},{56,48},{64,56},{72,6... | collective-permute-start | bytes 57608 | tf_op jit(solution)/shard_map/ppermute | solution.py:19
  28.9 5.9 %collective-permute-start.1 = (f32[150,32,2]{0,1,2:T(8,128)S(1)}, f32[150,32,2]{0,1,2:T(8,128)S(1)}, u32[]{:S(2)}, u32[]{:S(2)}) collective-permute-start(f32[150,32,2]{0,1,2:T(8,128)S(1)} %copy.81), channel_id=1, source_target_pairs={{8,0},{16,8},{24,16},{32,24},{40,32},{48,40},{56,48},{64,56},{72,6... | collective-permute-start | bytes 115208 | tf_op jit(solution)/shard_map/ppermute | solution.py:19
  56.6 4.0 copy.83
  79.6 21.7 %fusion.42 = (f32[150,32,128]{2,1,0:T(8,128)S(1)}, f32[150,32,128]{2,1,0:T(8,128)}, f32[150,32,128]{2,1,0:T(8,128)}, f32[150,32,128]{2,1,0:T(8,128)}, f32[150,32,128]{2,1,0:T(8,128)}) fusion(f32[150,32,128]{2,1,0:T(8,128)} %param.7, f32[150,32,1]{2,1,0:T(8,128)} %copy.89, f32[150,32,1]{2,1,0:T(8,128)} %copy.88, f32[150,1,130]{2,1,0:T(1,128)S(1)} %copy.95, ...), kind=kLoop, calls=%fused_computation.73 | loop fusion | flops 19660800 | bytes 17791200 | tf_op jit(solution)/shard_map/add | solution.py:43
  109.2 5.6 %collective-permute-start.9 = (f32[150,32,1]{0,1,2:T(8,128)S(1)}, f32[150,32,1]{0,1,2:T(8,128)S(1)}, u32[]{:S(2)}, u32[]{:S(2)}) collective-permute-start(f32[150,32,1]{0,1,2:T(8,128)S(1)} %copy.101), channel_id=1, source_target_pairs={{8,0},{16,8},{24,16},{32,24},{40,32},{48,40},{56,48},{64,56},{72,6... | collective-permute-start | bytes 57608 | tf_op jit(solution)/shard_map/ppermute | solution.py:19
  114.8 4.0 copy.102
  135.7 10.4 %fusion.30 = f32[150,32,128]{2,1,0:T(8,128)} fusion(f32[150,32,128]{2,1,0:T(8,128)S(1)} %copy-done.1, f32[150,32,128]{2,1,0:T(8,128)} %get-tuple-element.10, f32[150,32,1]{2,1,0:T(8,128)} %copy.103, f32[150,32,128]{2,1,0:T(8,128)} %get-tuple-element.9, f32[150,32,1]{2,1,0:T(8,128)} %copy.102, f32[150,32,128]{2,1,0:T(8,128)} %get-tuple-element.8, ...), kind=kLoop, calls=%fused_computation.53 | loop fusion | flops 12288000 | bytes 14940000 | tf_op jit(solution)/shard_map/add | solution.py:43
  146.1 5.0 %copy.134 = f32[150,32,128]{0,2,1:T(8,128)} copy(f32[150,32,128]{2,1,0:T(8,128)} %fusion.30) | data formatting | bytes 4915200 | tf_op jit(solution)/shard_map/reshape | solution.py:79
  151.1 4.4 concatenate.102
  155.5 12.0 %gather_fusion = f32[3072,150]{1,0:T(8,128)S(1)} fusion(f32[150,4097]{0,1:T(8,128)} %concatenate.102, s32[3072]{0:T(1024)S(1)} %broadcast_clamp_fusion.1), kind=kCustom, calls=%fused_computation | custom fusion | bytes 3698688 | tf_op jit(solution)/shard_map/jit(_take)/gather | solution.py:82
  169.5 7.3 %all-to-all-start = ((f32[150,128,24]{0,2,1:T(8,128)}), f32[150,128,24]{0,2,1:T(8,128)S(1)}, u32[]{:S(2)}, u32[]{:S(2)}) async-start(f32[150,128,24]{0,2,1:T(8,128)} %broadcast_select_fusion), calls=%async_computation | async-start | bytes 6291456 | tf_op jit(solution)/shard_map/all_to_all | solution.py:64
  176.9 40.8 %all-to-all-done = f32[150,128,24]{0,2,1:T(8,128)S(1)} async-done(((f32[150,128,24]{0,2,1:T(8,128)}), f32[150,128,24]{0,2,1:T(8,128)S(1)}, u32[]{:S(2)}, u32[]{:S(2)}) %all-to-all-start) | async-done | bytes 1843232 | tf_op jit(solution)/shard_map/all_to_all | solution.py:64
  217.7 31.5 %gather_fusion.1 = f32[8192,150]{1,0:T(8,128)} fusion(f32[150,3072]{0,1:T(8,128)S(1)} %bitcast.28, s32[8192]{0:T(1024)S(1)} %broadcast_clamp_fusion), kind=kCustom, calls=%fused_computation.1 | custom fusion | bytes 9863168 | tf_op jit(solution)/shard_map/jit(_take)/gather | solution.py:87
  249.2 7.2 %multiply_reduce_fusion = f32[150,2048]{0,1:T(8,128)S(1)} fusion(f32[150,4,2048]{0,2,1:T(8,128)} %bitcast.29, f32[4,2048]{1,0:T(4,128)S(1)} %copy-done.8, pred[4,2048]{1,0:T(4,128)(4,1)S(1)} %compare_and_fusion.1), kind=kLoop, calls=%fused_computation.7 | loop fusion | flops 3379200 | bytes 6184960 | tf_op jit(solution)/shard_map/reduce_sum | solution.py:88
  261.6 45.9 %scatter_custom_fusion = f32[150,3072]{0,1:T(8,128)S(1)} fusion(s32[8192]{0:T(1024)S(1)} %bitcast.40, f32[150,8192]{0,1:T(8,128)} %bitcast_multiply_fusion, f32[]{:T(128)} %constant.12.clone.1), kind=kCustom, calls=%fused_computation.4 | custom fusion | flops 1228800 | bytes 6758404 | tf_op jit(solution)/shard_map/scatter-add | solution.py:91
  307.5 46.0 %all_to_all.21 = f32[150,128,24]{0,2,1:T(8,128)} all-to-all(f32[150,128,24]{0,2,1:T(8,128)S(1)} %bitcast.32), channel_id=1, replica_groups=mesh['lon'=16,'lat'=8] {'lon','lat'}, dimensions={1} | all-to-all | bytes 3686400 | tf_op jit(solution)/shard_map/all_to_all | solution.py:68
  353.6 19.6 %scatter_custom_fusion.1 = f32[150,4097]{0,1:T(8,128)} fusion(s32[3072]{0:T(1024)S(1)} %bitcast.42, f32[3072,150]{1,0:T(8,128)} %bitcast.34, f32[]{:T(128)} %constant.12.clone.1), kind=kCustom, calls=%fused_computation.102 | custom fusion | flops 460800 | bytes 2458712 | tf_op jit(solution)/shard_map/scatter-add | solution.py:93
  373.2 4.5 slice.218
  391.9 5.4 %collective-permute-start.13 = (f32[150,32,1]{0,1,2:T(8,128)S(1)}, f32[150,32,1]{0,1,2:T(8,128)S(1)}, u32[]{:S(2)}, u32[]{:S(2)}) collective-permute-start(f32[150,32,1]{0,1,2:T(8,128)S(1)} %copy.114), channel_id=1, source_target_pairs={{8,0},{16,8},{24,16},{32,24},{40,32},{48,40},{56,48},{64,56},{72,6... | collective-permute-start | bytes 57608 | tf_op jit(solution)/shard_map/ppermute | solution.py:19
  415.1 4.3 collective-permute-done.15
  419.6 10.0 %fusion.18 = f32[150,32,128]{2,1,0:T(8,128)S(1)} fusion(f32[150,32,128]{2,1,0:T(8,128)S(1)} %copy.135, f32[150,32,128]{2,1,0:T(8,128)} %get-tuple-element.10, f32[150,32,1]{2,1,0:T(8,128)} %copy.116, f32[150,32,128]{2,1,0:T(8,128)} %get-tuple-element.9, f32[150,32,1]{2,1,0:T(8,128)} %copy.115, f32[150,32,128]{2,1,0:T(8,128)} %get-tuple-element.8, ...), kind=kLoop, calls=%fused_computation.33 | loop fusion | flops 12288000 | bytes 14940000 | tf_op jit(solution)/shard_map/add | solution.py:43
  437.7 5.4 %collective-permute-start.17 = (f32[150,32,1]{0,1,2:T(8,128)S(1)}, f32[150,32,1]{0,1,2:T(8,128)S(1)}, u32[]{:S(2)}, u32[]{:S(2)}) collective-permute-start(f32[150,32,1]{0,1,2:T(8,128)S(1)} %copy.124), channel_id=1, source_target_pairs={{8,0},{16,8},{24,16},{32,24},{40,32},{48,40},{56,48},{64,56},{72,6... | collective-permute-start | bytes 57608 | tf_op jit(solution)/shard_map/ppermute | solution.py:19
  464.6 16.1 %fusion.6 = f32[150,32,128]{2,1,0:T(8,128)} fusion(f32[150,32,128]{2,1,0:T(8,128)S(1)} %copy-done.2, f32[150,32,128]{2,1,0:T(8,128)} %copy-done.3, f32[150,32,128]{2,1,0:T(8,128)} %get-tuple-element.10, f32[150,32,1]{2,1,0:T(8,128)} %copy.126, f32[150,32,128]{2,1,0:T(8,128)} %get-tuple-element.9, f32[150,32,1]{2,1,0:T(8,128)} %copy.125, ...), kind=kLoop, calls=%fused_computation.13 | loop fusion | flops 12902400 | bytes 17397600 | tf_op jit(solution)/shard_map/add | solution.py:95
  (122 shorter events, 151.7 us)
Async XLA Ops:
  8.8 26.0 %collective-permute-start.3 = (f32[150,32,1]{0,1,2:T(8,128)S(1)}, f32[150,32,1]{0,1,2:T(8,128)S(1)}, u32[]{:S(2)}, u32[]{:S(2)}) collective-permute-start(f32[150,32,1]{0,1,2:T(8,128)S(1)} %copy.136), channel_id=1, source_target_pairs={{0,8},{8,16},{16,24},{24,32},{32,40},{40,48},{48,56},{56,64},{64,7... | collective-permute-start | bytes 57608 | tf_op jit(solution)/shard_map/ppermute | solution.py:17
  10.9 28.0 %collective-permute-start.4 = (f32[150,32,1]{0,1,2:T(8,128)S(1)}, f32[150,32,1]{0,1,2:T(8,128)S(1)}, u32[]{:S(2)}, u32[]{:S(2)}) collective-permute-start(f32[150,32,1]{0,1,2:T(8,128)S(1)} %copy.137), channel_id=1, source_target_pairs={{8,0},{16,8},{24,16},{32,24},{40,32},{48,40},{56,48},{64,56},{72,6... | collective-permute-start | bytes 57608 | tf_op jit(solution)/shard_map/ppermute | solution.py:19
  25.4 27.2 %collective-permute-start = (f32[150,32,2]{0,1,2:T(8,128)S(1)}, f32[150,32,2]{0,1,2:T(8,128)S(1)}, u32[]{:S(2)}, u32[]{:S(2)}) collective-permute-start(f32[150,32,2]{0,1,2:T(8,128)S(1)} %copy.80), channel_id=1, source_target_pairs={{0,8},{8,16},{16,24},{24,32},{32,40},{40,48},{48,56},{56,64},{64,7... | collective-permute-start | bytes 115208 | tf_op jit(solution)/shard_map/ppermute | solution.py:17
  28.9 27.7 %collective-permute-start.1 = (f32[150,32,2]{0,1,2:T(8,128)S(1)}, f32[150,32,2]{0,1,2:T(8,128)S(1)}, u32[]{:S(2)}, u32[]{:S(2)}) collective-permute-start(f32[150,32,2]{0,1,2:T(8,128)S(1)} %copy.81), channel_id=1, source_target_pairs={{8,0},{16,8},{24,16},{32,24},{40,32},{48,40},{56,48},{64,56},{72,6... | collective-permute-start | bytes 115208 | tf_op jit(solution)/shard_map/ppermute | solution.py:19
  46.0 26.4 %collective-permute-start.5 = (f32[150,1,130]{0,2,1:T(8,128)S(1)}, f32[150,1,130]{0,2,1:T(8,128)S(1)}, u32[]{:S(2)}, u32[]{:S(2)}) collective-permute-start(f32[150,1,130]{0,2,1:T(8,128)S(1)} %copy.90), channel_id=1, source_target_pairs={{1,0},{2,1},{3,2},{4,3},{5,4},{6,5},{7,6},{9,8},{10,9},{11,10},{12... | collective-permute-start | bytes 234008 | tf_op jit(solution)/shard_map/ppermute | solution.py:19
  49.5 23.1 %collective-permute-start.7 = (f32[150,1,130]{0,2,1:T(8,128)}, f32[150,1,130]{0,2,1:T(8,128)}, u32[]{:S(2)}, u32[]{:S(2)}) collective-permute-start(f32[150,1,130]{0,2,1:T(8,128)} %copy.94), channel_id=1, source_target_pairs={{0,1},{1,2},{2,3},{3,4},{4,5},{5,6},{6,7},{8,9},{9,10},{10,11},{11... | collective-permute-start | bytes 234008 | tf_op jit(solution)/shard_map/ppermute | solution.py:17
  60.7 10.5 %copy-start.10 = (s32[1,3072]{1,0:T(1,128)S(1)}, s32[1,3072]{1,0:T(1,128)}, u32[]{:S(2)}) copy-start(s32[1,3072]{1,0:T(1,128)} %param.10) | copy-start | bytes 36868
  64.3 10.5 %collective-permute-start.2 = (f32[150,2,132]{0,2,1:T(8,128)}, f32[150,2,132]{0,2,1:T(8,128)S(1)}, u32[]{:S(2)}, u32[]{:S(2)}) collective-permute-start(f32[150,2,132]{0,2,1:T(8,128)} %copy.84), channel_id=1, source_target_pairs={{1,0},{2,1},{3,2},{4,3},{5,4},{6,5},{7,6},{9,8},{10,9},{11,10},{12... | collective-permute-start | bytes 475208 | tf_op jit(solution)/shard_map/ppermute | solution.py:19
  68.7 9.6 %collective-permute-start.6 = (f32[150,2,132]{0,2,1:T(8,128)}, f32[150,2,132]{0,2,1:T(8,128)}, u32[]{:S(2)}, u32[]{:S(2)}) collective-permute-start(f32[150,2,132]{0,2,1:T(8,128)} %copy.92), channel_id=1, source_target_pairs={{0,1},{1,2},{2,3},{3,4},{4,5},{5,6},{6,7},{8,9},{9,10},{10,11},{11... | collective-permute-start | bytes 475208 | tf_op jit(solution)/shard_map/ppermute | solution.py:17
  107.1 7.7 %collective-permute-start.8 = (f32[150,32,1]{0,1,2:T(8,128)S(1)}, f32[150,32,1]{0,1,2:T(8,128)S(1)}, u32[]{:S(2)}, u32[]{:S(2)}) collective-permute-start(f32[150,32,1]{0,1,2:T(8,128)S(1)} %copy.100), channel_id=1, source_target_pairs={{0,8},{8,16},{16,24},{24,32},{32,40},{40,48},{48,56},{56,64},{64,7... | collective-permute-start | bytes 57608 | tf_op jit(solution)/shard_map/ppermute | solution.py:17
  109.2 9.7 %collective-permute-start.9 = (f32[150,32,1]{0,1,2:T(8,128)S(1)}, f32[150,32,1]{0,1,2:T(8,128)S(1)}, u32[]{:S(2)}, u32[]{:S(2)}) collective-permute-start(f32[150,32,1]{0,1,2:T(8,128)S(1)} %copy.101), channel_id=1, source_target_pairs={{8,0},{16,8},{24,16},{32,24},{40,32},{48,40},{56,48},{64,56},{72,6... | collective-permute-start | bytes 57608 | tf_op jit(solution)/shard_map/ppermute | solution.py:19
  125.7 8.8 %collective-permute-start.10 = (f32[150,1,130]{0,2,1:T(8,128)S(1)}, f32[150,1,130]{0,2,1:T(8,128)S(1)}, u32[]{:S(2)}, u32[]{:S(2)}) collective-permute-start(f32[150,1,130]{0,2,1:T(8,128)S(1)} %copy.104), channel_id=1, source_target_pairs={{1,0},{2,1},{3,2},{4,3},{5,4},{6,5},{7,6},{9,8},{10,9},{11,10},{12... | collective-permute-start | bytes 234008 | tf_op jit(solution)/shard_map/ppermute | solution.py:19
  127.7 7.8 %collective-permute-start.11 = (f32[150,1,130]{0,2,1:T(8,128)S(1)}, f32[150,1,130]{0,2,1:T(8,128)S(1)}, u32[]{:S(2)}, u32[]{:S(2)}) collective-permute-start(f32[150,1,130]{0,2,1:T(8,128)S(1)} %copy.106), channel_id=1, source_target_pairs={{0,1},{1,2},{2,3},{3,4},{4,5},{5,6},{6,7},{8,9},{9,10},{10,11},{11... | collective-permute-start | bytes 234008 | tf_op jit(solution)/shard_map/ppermute | solution.py:17
  169.5 48.2 %all-to-all-start = ((f32[150,128,24]{0,2,1:T(8,128)}), f32[150,128,24]{0,2,1:T(8,128)S(1)}, u32[]{:S(2)}, u32[]{:S(2)}) async-start(f32[150,128,24]{0,2,1:T(8,128)} %broadcast_select_fusion), calls=%async_computation | async-start | bytes 6291456 | tf_op jit(solution)/shard_map/all_to_all | solution.py:64
  388.1 9.1 %collective-permute-start.12 = (f32[150,32,1]{0,1,2:T(8,128)S(1)}, f32[150,32,1]{0,1,2:T(8,128)S(1)}, u32[]{:S(2)}, u32[]{:S(2)}) collective-permute-start(f32[150,32,1]{0,1,2:T(8,128)S(1)} %copy.113), channel_id=1, source_target_pairs={{0,8},{8,16},{16,24},{24,32},{32,40},{40,48},{48,56},{56,64},{64,7... | collective-permute-start | bytes 57608 | tf_op jit(solution)/shard_map/ppermute | solution.py:17
  391.9 9.4 %collective-permute-start.13 = (f32[150,32,1]{0,1,2:T(8,128)S(1)}, f32[150,32,1]{0,1,2:T(8,128)S(1)}, u32[]{:S(2)}, u32[]{:S(2)}) collective-permute-start(f32[150,32,1]{0,1,2:T(8,128)S(1)} %copy.114), channel_id=1, source_target_pairs={{8,0},{16,8},{24,16},{32,24},{40,32},{48,40},{56,48},{64,56},{72,6... | collective-permute-start | bytes 57608 | tf_op jit(solution)/shard_map/ppermute | solution.py:19
  408.1 6.9 %collective-permute-start.14 = (f32[150,1,130]{0,2,1:T(8,128)S(1)}, f32[150,1,130]{0,2,1:T(8,128)S(1)}, u32[]{:S(2)}, u32[]{:S(2)}) collective-permute-start(f32[150,1,130]{0,2,1:T(8,128)S(1)} %copy.117), channel_id=1, source_target_pairs={{1,0},{2,1},{3,2},{4,3},{5,4},{6,5},{7,6},{9,8},{10,9},{11,10},{12... | collective-permute-start | bytes 234008 | tf_op jit(solution)/shard_map/ppermute | solution.py:19
  411.6 7.8 %collective-permute-start.15 = (f32[150,1,130]{0,2,1:T(8,128)S(1)}, f32[150,1,130]{0,2,1:T(8,128)S(1)}, u32[]{:S(2)}, u32[]{:S(2)}) collective-permute-start(f32[150,1,130]{0,2,1:T(8,128)S(1)} %copy.119), channel_id=1, source_target_pairs={{0,1},{1,2},{2,3},{3,4},{4,5},{5,6},{6,7},{8,9},{9,10},{10,11},{11... | collective-permute-start | bytes 234008 | tf_op jit(solution)/shard_map/ppermute | solution.py:17
  435.4 7.7 %collective-permute-start.16 = (f32[150,32,1]{0,1,2:T(8,128)S(1)}, f32[150,32,1]{0,1,2:T(8,128)S(1)}, u32[]{:S(2)}, u32[]{:S(2)}) collective-permute-start(f32[150,32,1]{0,1,2:T(8,128)S(1)} %copy.123), channel_id=1, source_target_pairs={{0,8},{8,16},{16,24},{24,32},{32,40},{40,48},{48,56},{56,64},{64,7... | collective-permute-start | bytes 57608 | tf_op jit(solution)/shard_map/ppermute | solution.py:17
  437.7 13.5 %copy-start.4 = (f32[150,32,128]{2,1,0:T(8,128)S(1)}, f32[150,32,128]{2,1,0:T(8,128)}, u32[]{:S(2)}) copy-start(f32[150,32,128]{2,1,0:T(8,128)} %copy-done.3) | copy-start | bytes 7372804
  437.7 9.4 %collective-permute-start.17 = (f32[150,32,1]{0,1,2:T(8,128)S(1)}, f32[150,32,1]{0,1,2:T(8,128)S(1)}, u32[]{:S(2)}, u32[]{:S(2)}) collective-permute-start(f32[150,32,1]{0,1,2:T(8,128)S(1)} %copy.124), channel_id=1, source_target_pairs={{8,0},{16,8},{24,16},{32,24},{40,32},{48,40},{56,48},{64,56},{72,6... | collective-permute-start | bytes 57608 | tf_op jit(solution)/shard_map/ppermute | solution.py:19
  453.8 10.8 %copy-start.2 = (f32[150,32,128]{2,1,0:T(8,128)S(1)}, f32[150,32,128]{2,1,0:T(8,128)}, u32[]{:S(2)}) copy-start(f32[150,32,128]{2,1,0:T(8,128)} %param.7) | copy-start | bytes 7372804
  453.9 8.8 %collective-permute-start.18 = (f32[150,1,130]{0,2,1:T(8,128)S(1)}, f32[150,1,130]{0,2,1:T(8,128)S(1)}, u32[]{:S(2)}, u32[]{:S(2)}) collective-permute-start(f32[150,1,130]{0,2,1:T(8,128)S(1)} %copy.127), channel_id=1, source_target_pairs={{1,0},{2,1},{3,2},{4,3},{5,4},{6,5},{7,6},{9,8},{10,9},{11,10},{12... | collective-permute-start | bytes 234008 | tf_op jit(solution)/shard_map/ppermute | solution.py:19
  456.6 7.8 %collective-permute-start.19 = (f32[150,1,130]{0,2,1:T(8,128)S(1)}, f32[150,1,130]{0,2,1:T(8,128)S(1)}, u32[]{:S(2)}, u32[]{:S(2)}) collective-permute-start(f32[150,1,130]{0,2,1:T(8,128)S(1)} %copy.129), channel_id=1, source_target_pairs={{0,1},{1,2},{2,3},{3,4},{4,5},{5,6},{6,7},{8,9},{9,10},{10,11},{11... | collective-permute-start | bytes 234008 | tf_op jit(solution)/shard_map/ppermute | solution.py:17
  (8 other events, 46.3 us)
where the time goes:
time: 490 us; the launch traced here: 481 us
  local copies, waits for them, and re-layouts  161 us (33%)
  other arithmetic  153 us (31%)
  starting transfers between devices  65.7 us (13%)
  waiting for transfers between devices  53.2 us (11%)
  blocking collectives  46 us (9%)
    all_to_all x1, blocking collectives, to_sources(): lax.all_to_all(returned, ('lon', 'lat'), split_axis=1, concat_axis=1, til...  46 us
    scatter-add x1, other arithmetic, on_device(): jnp.zeros((vals, slot_count), jnp.float32).at[:, all_slots].add(spread)  45.9 us
    ppermute x10, starting transfers between devices, with_halo(): lax.ppermute(head, axis, [((i + 1) % count, i) for i in range(ends)])  42.4 us
    add x3, other arithmetic, relax_step(): return centre + total  42.1 us
    all_to_all x1, waiting for transfers between devices, to_owners(): lax.all_to_all(outgoing, ('lon', 'lat'), split_axis=1, concat_axis=1, til...  40.8 us
    gather x1, local copies, waits for them, and re-layouts, on_device(): jnp.take(received, all_slots, axis=1).reshape(vals, taps, obs_count)  31.5 us
    slice x14, local copies, waits for them, and re-layouts, with_halo(): lax.slice_in_dim(cells, cells.shape[dim] - width, cells.shape[dim], axis=...  31.5 us
    ppermute x10, local copies, waits for them, and re-layouts, with_halo(): lax.ppermute(tail, axis, [(i, (i + 1) % count) for i in range(ends)])  22.7 us
  transfers between devices with their start and end apart: 21, of which 7 were waited for; matrix products, arithmetic and copies ran while one was open for 14% of the time, Pallas kernels for 0%

commit v1 on v0

v1 whole, which is shorter than its diff:
```python
import functools

import jax
import jax.numpy as jnp
from jax import lax
from jax.experimental import pallas as pl
from jax.experimental.pallas import tpu as pltpu
from jax.sharding import PartitionSpec as P

SWEEPS = 2
GROUP = 30


def shift_lat(edge, down):
    count = lax.axis_size("lat")
    if down:
        pairs = [(i, i + 1) for i in range(count - 1)]
    else:
        pairs = [(i + 1, i) for i in range(count - 1)]
    return lax.ppermute(edge, "lat", pairs)


def shift_lon(edge, east):
    count = lax.axis_size("lon")
    if east:
        pairs = [(i, (i + 1) % count) for i in range(count)]
    else:
        pairs = [((i + 1) % count, i) for i in range(count)]
    return lax.ppermute(edge, "lon", pairs)


def halos(top, bottom, left, right):
    return (
        shift_lat(bottom, True),
        shift_lat(top, False),
        shift_lon(right, True),
        shift_lon(left, False),
    )


def sweep_kernel(rows, v_ref, c_ref, vn_ref, vs_ref, vw_ref, ve_ref, cn_ref, cs_ref, cw_ref, ce_ref,
                 w_ref, top_ref, bot_ref, left_ref, right_ref):
    group = vn_ref.shape[1]
    lanes = v_ref.shape[2]
    lane = lax.broadcasted_iota(jnp.int32, (group, lanes), 1)
    col = lax.broadcasted_iota(jnp.int32, (group, rows), 1)

    def slab(ref, r):
        return ref[0, pl.ds(r, group, stride=rows), :]

    vw = vw_ref[0]
    ve = ve_ref[0]
    cw = cw_ref[0]
    ce = ce_ref[0]
    left = jnp.zeros((group, rows), jnp.float32)
    right = jnp.zeros((group, rows), jnp.float32)
    x_up, c_up = vn_ref[0], cn_ref[0]
    x_mid, c_mid = slab(v_ref, 0), slab(c_ref, 0)
    for r in range(rows):
        if r + 1 < rows:
            x_dn, c_dn = slab(v_ref, r + 1), slab(c_ref, r + 1)
        else:
            x_dn, c_dn = vs_ref[0], cs_ref[0]
        x_w = jnp.where(lane == 0, vw[:, r : r + 1], pltpu.roll(x_mid, 1, 1))
        x_e = jnp.where(lane == lanes - 1, ve[:, r : r + 1], pltpu.roll(x_mid, lanes - 1, 1))
        c_w = jnp.where(lane == 0, cw[:, r : r + 1], pltpu.roll(c_mid, 1, 1))
        c_e = jnp.where(lane == lanes - 1, ce[:, r : r + 1], pltpu.roll(c_mid, lanes - 1, 1))
        total = jnp.minimum(c_mid, c_up) * (x_up - x_mid)
        total = total + jnp.minimum(c_mid, c_dn) * (x_dn - x_mid)
        total = total + jnp.minimum(c_mid, c_w) * (x_w - x_mid)
        total = total + jnp.minimum(c_mid, c_e) * (x_e - x_mid)
        out = x_mid + total
        w_ref[0, pl.ds(r, group, stride=rows), :] = out
        if r == 0:
            top_ref[0] = out
        if r == rows - 1:
            bot_ref[0] = out
        left = jnp.where(col == r, out[:, 0:1], left)
        right = jnp.where(col == r, out[:, lanes - 1 : lanes], right)
        x_up, c_up = x_mid, c_mid
        x_mid, c_mid = x_dn, c_dn
    left_ref[0] = left
    right_ref[0] = right


def sweep(field, conduct, field_halos, coef_halos):
    steps, span, lanes = field.shape
    rows = span // GROUP
    big = pl.BlockSpec((1, span, lanes), lambda i: (i, 0, 0))
    row_edge = pl.BlockSpec((1, GROUP, lanes), lambda i: (i, 0, 0))
    col_edge = pl.BlockSpec((1, GROUP, rows), lambda i: (i, 0, 0))
    edge_specs = [row_edge, row_edge, col_edge, col_edge]
    return pl.pallas_call(
        functools.partial(sweep_kernel, rows),
        grid=(steps,),
        in_specs=[big, big] + edge_specs + edge_specs,
        out_specs=[big] + edge_specs,
        out_shape=[
            jax.ShapeDtypeStruct(field.shape, jnp.float32),
            jax.ShapeDtypeStruct((steps, GROUP, lanes), jnp.float32),
            jax.ShapeDtypeStruct((steps, GROUP, lanes), jnp.float32),
            jax.ShapeDtypeStruct((steps, GROUP, rows), jnp.float32),
            jax.ShapeDtypeStruct((steps, GROUP, rows), jnp.float32),
        ],
        cost_estimate=pl.CostEstimate(
            flops=20 * field.size, bytes_accessed=12 * field.size, transcendentals=0
        ),
    )(field, conduct, *field_halos, *coef_halos)


def edges_of(field):
    vals, rows, lanes = field.shape
    steps = vals // GROUP
    top = field[:, 0, :].reshape(steps, GROUP, lanes)
    bottom = field[:, rows - 1, :].reshape(steps, GROUP, lanes)
    left = field[:, :, 0].reshape(steps, GROUP, rows)
    right = field[:, :, lanes - 1].reshape(steps, GROUP, rows)
    return top, bottom, left, right


def diffuse(field, conduct_blocks, coef_halos):
    vals, rows, lanes = field.shape
    steps = vals // GROUP
    edges = edges_of(field)
    current = field.reshape(steps, GROUP * rows, lanes)
    for _ in range(SWEEPS):
        current, *edges = sweep(current, conduct_blocks, halos(*edges), coef_halos)
    return current.reshape(vals, rows, lanes)


def to_owners(outgoing):
    return lax.all_to_all(outgoing, ("lon", "lat"), split_axis=1, concat_axis=1, tiled=True)


def to_sources(returned):
    return lax.all_to_all(returned, ("lon", "lat"), split_axis=1, concat_axis=1, tiled=True)


def on_device(state, diffusivity, sea_mask, send_cols, obs_slots, obs_weights, obs_precision):
    vals, rows, lanes = state.shape
    cell_count = rows * lanes
    steps = vals // GROUP
    sea_float = sea_mask.astype(jnp.float32)
    conduct = diffusivity * jnp.concatenate([sea_float, sea_float], axis=0)
    coef_halos = halos(*edges_of(conduct))
    conduct_blocks = conduct.reshape(steps, GROUP * rows, lanes)
    smooth = diffuse(state, conduct_blocks, coef_halos)
    flat_cols = jnp.concatenate(
        [smooth.reshape(vals, cell_count), jnp.zeros((vals, 1), jnp.float32)], axis=1
    )
    send_index = send_cols[0]
    outgoing = jnp.take(flat_cols, send_index, axis=1)
    received = to_owners(outgoing)
    slot_count = outgoing.shape[1]
    taps, obs_count = obs_slots.shape
    all_slots = obs_slots.reshape(taps * obs_count)
    picked = jnp.take(received, all_slots, axis=1).reshape(vals, taps, obs_count)
    equivalents = jnp.sum(picked * obs_weights[None, :, :], axis=1)
    weighted = obs_precision * equivalents
    spread = (weighted[:, None, :] * obs_weights[None, :, :]).reshape(vals, taps * obs_count)
    returned = jnp.zeros((vals, slot_count), jnp.float32).at[:, all_slots].add(spread)
    incoming = to_sources(returned)
    adjoint_cols = jnp.zeros((vals, cell_count + 1), jnp.float32).at[:, send_index].add(incoming)
    adjoint_field = adjoint_cols[:, :cell_count].reshape(state.shape)
    product = state + diffuse(adjoint_field, conduct_blocks, coef_halos)
    return (product, equivalents)


def solution(mesh):
    placed = (
        P(None, "lat", "lon"),
        P(None, "lat", "lon"),
        P(None, "lat", "lon"),
        P(("lon", "lat"), None),
        P(None, ("lon", "lat")),
        P(None, ("lon", "lat")),
        P(None, ("lon", "lat")),
    )
    return jax.shard_map(
        on_device,
        mesh=mesh,
        in_specs=placed,
        out_specs=(P(None, "lat", "lon"), P(None, ("lon", "lat"))),
        check_vma=False,
    )
```

time: 490 us -> 423 us (0.86); the launches traced: 481 us -> 421 us
  Pallas kernels: 0 us -> 88.2 us
  local copies, waits for them, and re-layouts: 161 us -> 85.5 us
  other arithmetic: 153 us -> 86.3 us
  waiting for transfers between devices: 53.2 us -> 44.4 us
    pallas_call x0 -> x4, Pallas kernels: none -> 88.2 us  [sweep(): pl.pallas_call(functools.partial(sweep_kernel, rows), grid=(steps,), in_s...]
    add x4 -> x1, other arithmetic: 58.2 us -> 3.7 us  [on_device(): product = state + diffuse(adjoint_field, conduct_blocks, coef_halos)]
    ppermute x20 -> x0, local copies, waits for them, and re-layouts: 43.5 us -> none  [the longest x10 22.7 us: with_halo(): lax.ppermute(tail, axis, [(i, (i + 1) % count) for i in range(ends)])]
    slice x23 -> x6, local copies, waits for them, and re-layouts: 43.8 us -> 9.68 us  [the longest x3 7.6 us: edges_of(): left = field[:, :, 0].reshape(steps, GROUP, rows)]
    slice x4 -> x0, other arithmetic: 11.1 us -> none  [with_halo(): head = lax.slice_in_dim(cells, 0, width, axis=dim)]
    another operation x0 -> x15, local copies, waits for them, and re-layouts: none -> 10.3 us  [the longest x2 5.96 us: on_device(): smooth.reshape(vals, cell_count)]
    ppermute x20, waiting for transfers between devices: 12.4 us -> 3.41 us  [the longest x10 2.83 us: shift_lon(): return lax.ppermute(edge, 'lon', pairs)]
    reshape x2 -> x0, local copies, waits for them, and re-layouts: 8.81 us -> none  [the longest x1 5 us: on_device(): smooth.reshape(vals, cell_count)]
  transfers between devices with their start and end apart: 21 -> 21, of which waited for: 7 -> 4; matrix products, arithmetic and copies ran while one was open for 14% -> 6% of each run, Pallas kernels for 0% -> 0%
where the time goes in v1:
time: 423 us; the launch traced here: 421 us
  Pallas kernels  88.2 us (21%)
  other arithmetic  86.3 us (20%)
  local copies, waits for them, and re-layouts  85.5 us (20%)
  starting transfers between devices  68.8 us (16%)
  blocking collectives  47 us (11%)
  waiting for transfers between devices  44.4 us (10%)
    pallas_call x4, Pallas kernels, sweep(): pl.pallas_call(functools.partial(sweep_kernel, rows), grid=(steps,), in_s...  88.2 us
    scatter-add x1, other arithmetic, on_device(): jnp.zeros((vals, slot_count), jnp.float32).at[:, all_slots].add(spread)  47 us
    all_to_all x1, blocking collectives, to_sources(): lax.all_to_all(returned, ('lon', 'lat'), split_axis=1, concat_axis=1, til...  47 us
    all_to_all x1, waiting for transfers between devices, to_owners(): lax.all_to_all(outgoing, ('lon', 'lat'), split_axis=1, concat_axis=1, til...  40.9 us
    ppermute x10, starting transfers between devices, shift_lat(): return lax.ppermute(edge, 'lat', pairs)  33.9 us
    gather x1, local copies, waits for them, and re-layouts, on_device(): jnp.take(received, all_slots, axis=1).reshape(vals, taps, obs_count)  31.5 us
    ppermute x10, starting transfers between devices, shift_lon(): return lax.ppermute(edge, 'lon', pairs)  26.8 us
    scatter-add x1, other arithmetic, on_device(): jnp.zeros((vals, cell_count + 1), jnp.float32).at[:, send_index]  19.6 us
  transfers between devices with their start and end apart: 21, of which 4 were waited for; matrix products, arithmetic and copies ran while one was open for 6% of the time, Pallas kernels for 0%

profile of v1, /device:TPU:8, one launch (start us, length us, event | category | flops | bytes accessed | tf_op | source)
XLA Modules:
  0.0 421.5 jit_solution(14360380380883552863)
XLA Ops:
  13.0 5.4 %collective-permute-start.7 = (f32[5,30,32]{2,1,0:T(8,128)S(1)}, f32[5,30,32]{2,1,0:T(8,128)S(1)}, u32[]{:S(2)}, u32[]{:S(2)}) collective-permute-start(f32[5,30,32]{2,1,0:T(8,128)S(1)} %reshape_squeeze.43), channel_id=1, source_target_pairs={{8,0},{16,8},{24,16},{32,24},{40,32},{48,40},{56,48},{64,56},{72,6... | collective-permute-start | bytes 57608 | tf_op jit(solution)/shard_map/ppermute | solution.py:29
  18.4 4.5 %slice_reduce_fusion.2 = (f32[150,32]{1,0:T(8,128)S(1)}, f32[150,32]{1,0:T(8,128)S(1)}) fusion(f32[150,32,128]{2,1,0:T(8,128)} %param.7), kind=kLoop, calls=%fused_computation.11 | loop fusion | bytes 76800 | tf_op jit(solution)/shard_map/slice | solution.py:116
  28.6 4.3 %collective-permute-start.1 = (f32[5,30,128]{2,1,0:T(8,128)S(1)}, f32[5,30,128]{2,1,0:T(8,128)S(1)}, u32[]{:S(2)}, u32[]{:S(2)}) collective-permute-start(f32[5,30,128]{2,1,0:T(8,128)S(1)} %reshape_squeeze.37), channel_id=1, source_target_pairs={{1,0},{2,1},{3,2},{4,3},{5,4},{6,5},{7,6},{9,8},{10,9},{11,10},{12... | collective-permute-start | bytes 230408 | tf_op jit(solution)/shard_map/ppermute | solution.py:20
  32.9 4.8 %collective-permute-start.3 = (f32[5,30,32]{2,1,0:T(8,128)S(1)}, f32[5,30,32]{2,1,0:T(8,128)S(1)}, u32[]{:S(2)}, u32[]{:S(2)}) collective-permute-start(f32[5,30,32]{2,1,0:T(8,128)S(1)} %reshape_squeeze.39), channel_id=1, source_target_pairs={{8,0},{16,8},{24,16},{32,24},{40,32},{48,40},{56,48},{64,56},{72,6... | collective-permute-start | bytes 57608 | tf_op jit(solution)/shard_map/ppermute | solution.py:29
  40.6 22.1 %shard_map.86 = (f32[5,960,128]{2,1,0:T(8,128)}, f32[5,30,128]{2,1,0:T(8,128)}, f32[5,30,128]{2,1,0:T(8,128)}, f32[5,30,32]{2,1,0:T(8,128)}, f32[5,30,32]{2,1,0:T(8,128)}) custom-call(f32[5,960,128]{2,1,0:T(8,128)} %bitcast.43, f32[5,960,128]{2,1,0:T(8,128)} %bitcast.39, f32[5,30,128]{2,1,0:T(8,128)} %copy-done.15, f32[5,30,128]{2,1,0:T(8,128)} %copy-done.19, ...), custom_call_target="tpu_custom_call" | custom-call | flops 12288000 | bytes 7372800 | tf_op jit(solution)/shard_map/pallas_call | solution.py:93
  62.7 5.5 %collective-permute-start.11 = (f32[5,30,32]{2,1,0:T(8,128)}, f32[5,30,32]{2,1,0:T(8,128)S(1)}, u32[]{:S(2)}, u32[]{:S(2)}) collective-permute-start(f32[5,30,32]{2,1,0:T(8,128)} %get-tuple-element.18), channel_id=1, source_target_pairs={{8,0},{16,8},{24,16},{32,24},{40,32},{48,40},{56,48},{64,56},{72,6... | collective-permute-start | bytes 57608 | tf_op jit(solution)/shard_map/ppermute | solution.py:29
  70.1 5.0 %collective-permute-start.9 = (f32[5,30,128]{2,1,0:T(8,128)}, f32[5,30,128]{2,1,0:T(8,128)S(1)}, u32[]{:S(2)}, u32[]{:S(2)}) collective-permute-start(f32[5,30,128]{2,1,0:T(8,128)} %get-tuple-element.16), channel_id=1, source_target_pairs={{1,0},{2,1},{3,2},{4,3},{5,4},{6,5},{7,6},{9,8},{10,9},{11,10},{12... | collective-permute-start | bytes 230408 | tf_op jit(solution)/shard_map/ppermute | solution.py:20
  78.3 22.1 %shard_map.87 = (f32[5,960,128]{2,1,0:T(8,128)}, f32[5,30,128]{2,1,0:T(8,128)}, f32[5,30,128]{2,1,0:T(8,128)}, f32[5,30,32]{2,1,0:T(8,128)}, f32[5,30,32]{2,1,0:T(8,128)}) custom-call(f32[5,960,128]{2,1,0:T(8,128)} %get-tuple-element.14.v_ref, f32[5,960,128]{2,1,0:T(8,128)} %bitcast.40, f32[5,30,128]{2,1,0:T(8,128)} %copy-done.23, f32[5,30,128]{2,1,0:T(8,128)} %copy-done.26, ...), custom_call_target="tpu_custom_call" | custom-call | flops 12288000 | bytes 7372800 | tf_op jit(solution)/shard_map/pallas_call | solution.py:93
  106.3 4.4 %concatenate.7 = f32[150,4097]{0,1:T(8,128)} pad(f32[150,4096]{0,1:T(8,128)} %copy.23, f32[]{:T(128)} %constant.12.clone.1), padding=0_0x0_1 | pad | bytes 4915804 | tf_op jit(solution)/shard_map/concatenate | solution.py:148
  110.7 12.0 %gather_fusion = f32[3072,150]{1,0:T(8,128)S(1)} fusion(f32[150,4097]{0,1:T(8,128)} %concatenate.7, s32[3072]{0:T(1024)S(1)} %broadcast_clamp_fusion.1), kind=kCustom, calls=%fused_computation | custom fusion | bytes 3698688 | tf_op jit(solution)/shard_map/jit(_take)/gather | solution.py:152
  124.7 8.1 %all-to-all-start = ((f32[150,128,24]{0,2,1:T(8,128)}), f32[150,128,24]{0,2,1:T(8,128)S(1)}, u32[]{:S(2)}, u32[]{:S(2)}) async-start(f32[150,128,24]{0,2,1:T(8,128)} %broadcast_select_fusion), calls=%async_computation | async-start | bytes 6291456 | tf_op jit(solution)/shard_map/all_to_all | solution.py:132
  132.9 40.9 %all-to-all-done = f32[150,128,24]{0,2,1:T(8,128)S(1)} async-done(((f32[150,128,24]{0,2,1:T(8,128)}), f32[150,128,24]{0,2,1:T(8,128)S(1)}, u32[]{:S(2)}, u32[]{:S(2)}) %all-to-all-start) | async-done | bytes 1843232 | tf_op jit(solution)/shard_map/all_to_all | solution.py:132
  173.8 31.5 %gather_fusion.1 = f32[8192,150]{1,0:T(8,128)} fusion(f32[150,3072]{0,1:T(8,128)S(1)} %bitcast.38, s32[8192]{0:T(1024)S(1)} %broadcast_clamp_fusion), kind=kCustom, calls=%fused_computation.1 | custom fusion | bytes 9863168 | tf_op jit(solution)/shard_map/jit(_take)/gather | solution.py:157
  205.3 7.2 %multiply_reduce_fusion = f32[150,2048]{0,1:T(8,128)S(1)} fusion(f32[150,4,2048]{0,2,1:T(8,128)} %bitcast.44, f32[4,2048]{1,0:T(4,128)S(1)} %copy-done.10, pred[4,2048]{1,0:T(4,128)(4,1)S(1)} %compare_and_fusion.1), kind=kLoop, calls=%fused_computation.7 | loop fusion | flops 3379200 | bytes 6184960 | tf_op jit(solution)/shard_map/reduce_sum | solution.py:158
  216.7 47.0 %scatter_custom_fusion = f32[150,3072]{0,1:T(8,128)} fusion(s32[8192]{0:T(1024)S(1)} %bitcast.56, f32[150,8192]{0,1:T(8,128)} %bitcast_multiply_fusion, f32[]{:T(128)} %constant.12.clone.1), kind=kCustom, calls=%fused_computation.4 | custom fusion | flops 1228800 | bytes 6758404 | tf_op jit(solution)/shard_map/scatter-add | solution.py:161
  263.7 47.0 %all_to_all.21 = f32[150,128,24]{0,2,1:T(8,128)} all-to-all(f32[150,128,24]{0,2,1:T(8,128)} %bitcast.47), channel_id=1, replica_groups=mesh['lon'=16,'lat'=8] {'lon','lat'}, dimensions={1} | all-to-all | bytes 3686400 | tf_op jit(solution)/shard_map/all_to_all | solution.py:136
  310.6 19.6 %scatter_custom_fusion.1 = f32[150,4097]{0,1:T(8,128)} fusion(s32[3072]{0:T(1024)} %bitcast.58, f32[3072,150]{1,0:T(8,128)} %bitcast.49, f32[]{:T(128)} %constant.12.clone.1), kind=kCustom, calls=%fused_computation.13 | custom fusion | flops 460800 | bytes 2458712 | tf_op jit(solution)/shard_map/scatter-add | solution.py:163
  337.5 4.2 collective-permute-start.13
  343.0 5.4 %collective-permute-start.15 = (f32[5,30,32]{2,1,0:T(8,128)S(1)}, f32[5,30,32]{2,1,0:T(8,128)S(1)}, u32[]{:S(2)}, u32[]{:S(2)}) collective-permute-start(f32[5,30,32]{2,1,0:T(8,128)S(1)} %reshape_squeeze.47), channel_id=1, source_target_pairs={{8,0},{16,8},{24,16},{32,24},{40,32},{48,40},{56,48},{64,56},{72,6... | collective-permute-start | bytes 57608 | tf_op jit(solution)/shard_map/ppermute | solution.py:29
  348.5 5.0 %copy.25 = f32[150,4096]{1,0:T(8,128)} copy(f32[150,4096]{0,1:T(8,128)} %copy-done.2) | data formatting | bytes 4915200 | tf_op jit(solution)/shard_map/slice | solution.py:164
  358.4 22.0 %shard_map.88 = (f32[5,960,128]{2,1,0:T(8,128)}, f32[5,30,128]{2,1,0:T(8,128)}, f32[5,30,128]{2,1,0:T(8,128)}, f32[5,30,32]{2,1,0:T(8,128)}, f32[5,30,32]{2,1,0:T(8,128)}) custom-call(f32[5,960,128]{2,1,0:T(8,128)} %reshape_reshape.7.v_ref, f32[5,960,128]{2,1,0:T(8,128)} %bitcast.41, f32[5,30,128]{2,1,0:T(8,128)} %copy-done.13, f32[5,30,128]{2,1,0:T(8,128)} %copy-done.14, ...), custom_call_target="tpu_custom_call" | custom-call | flops 12288000 | bytes 7372800 | tf_op jit(solution)/shard_map/pallas_call | solution.py:93
  382.4 4.8 %collective-permute-start.17 = (f32[5,30,128]{2,1,0:T(8,128)}, f32[5,30,128]{2,1,0:T(8,128)S(1)}, u32[]{:S(2)}, u32[]{:S(2)}) collective-permute-start(f32[5,30,128]{2,1,0:T(8,128)} %get-tuple-element.22), channel_id=1, source_target_pairs={{1,0},{2,1},{3,2},{4,3},{5,4},{6,5},{7,6},{9,8},{10,9},{11,10},{12... | collective-permute-start | bytes 230408 | tf_op jit(solution)/shard_map/ppermute | solution.py:20
  387.3 5.3 %collective-permute-start.19 = (f32[5,30,32]{2,1,0:T(8,128)}, f32[5,30,32]{2,1,0:T(8,128)S(1)}, u32[]{:S(2)}, u32[]{:S(2)}) collective-permute-start(f32[5,30,32]{2,1,0:T(8,128)} %get-tuple-element.24), channel_id=1, source_target_pairs={{8,0},{16,8},{24,16},{32,24},{40,32},{48,40},{56,48},{64,56},{72,6... | collective-permute-start | bytes 57608 | tf_op jit(solution)/shard_map/ppermute | solution.py:29
  395.7 22.1 %shard_map.89 = (f32[5,960,128]{2,1,0:T(8,128)}, f32[5,30,128]{2,1,0:T(8,128)}, f32[5,30,128]{2,1,0:T(8,128)}, f32[5,30,32]{2,1,0:T(8,128)}, f32[5,30,32]{2,1,0:T(8,128)}) custom-call(f32[5,960,128]{2,1,0:T(8,128)} %get-tuple-element.20.v_ref, f32[5,960,128]{2,1,0:T(8,128)} %bitcast.42, f32[5,30,128]{2,1,0:T(8,128)} %copy-done.16, f32[5,30,128]{2,1,0:T(8,128)} %copy-done.18, ...), custom_call_target="tpu_custom_call" | custom-call | flops 12288000 | bytes 7372800 | tf_op jit(solution)/shard_map/pallas_call | solution.py:93
  (135 shorter events, 59.9 us)
Async XLA Ops:
  3.6 36.3 %collective-permute-start.4 = (f32[5,30,128]{2,1,0:T(8,128)S(1)}, f32[5,30,128]{2,1,0:T(8,128)S(1)}, u32[]{:S(2)}, u32[]{:S(2)}) collective-permute-start(f32[5,30,128]{2,1,0:T(8,128)S(1)} %reshape_squeeze.40), channel_id=1, source_target_pairs={{0,1},{1,2},{2,3},{3,4},{4,5},{5,6},{6,7},{8,9},{9,10},{10,11},{11... | collective-permute-start | bytes 230408 | tf_op jit(solution)/shard_map/ppermute | solution.py:20
  7.0 32.8 %collective-permute-start.5 = (f32[5,30,128]{2,1,0:T(8,128)S(1)}, f32[5,30,128]{2,1,0:T(8,128)S(1)}, u32[]{:S(2)}, u32[]{:S(2)}) collective-permute-start(f32[5,30,128]{2,1,0:T(8,128)S(1)} %reshape_squeeze.41), channel_id=1, source_target_pairs={{1,0},{2,1},{3,2},{4,3},{5,4},{6,5},{7,6},{9,8},{10,9},{11,10},{12... | collective-permute-start | bytes 230408 | tf_op jit(solution)/shard_map/ppermute | solution.py:20
  13.0 13.1 %collective-permute-start.6 = (f32[5,30,32]{2,1,0:T(8,128)}, f32[5,30,32]{2,1,0:T(8,128)S(1)}, u32[]{:S(2)}, u32[]{:S(2)}) collective-permute-start(f32[5,30,32]{2,1,0:T(8,128)} %reshape_squeeze.42), channel_id=1, source_target_pairs={{0,8},{8,16},{16,24},{24,32},{32,40},{40,48},{48,56},{56,64},{64,7... | collective-permute-start | bytes 57608 | tf_op jit(solution)/shard_map/ppermute | solution.py:29
  13.0 15.6 %collective-permute-start.7 = (f32[5,30,32]{2,1,0:T(8,128)S(1)}, f32[5,30,32]{2,1,0:T(8,128)S(1)}, u32[]{:S(2)}, u32[]{:S(2)}) collective-permute-start(f32[5,30,32]{2,1,0:T(8,128)S(1)} %reshape_squeeze.43), channel_id=1, source_target_pairs={{8,0},{16,8},{24,16},{32,24},{40,32},{48,40},{56,48},{64,56},{72,6... | collective-permute-start | bytes 57608 | tf_op jit(solution)/shard_map/ppermute | solution.py:29
  23.0 9.9 %collective-permute-start.2 = (f32[5,30,32]{2,1,0:T(8,128)S(1)}, f32[5,30,32]{2,1,0:T(8,128)S(1)}, u32[]{:S(2)}, u32[]{:S(2)}) collective-permute-start(f32[5,30,32]{2,1,0:T(8,128)S(1)} %reshape_squeeze.38), channel_id=1, source_target_pairs={{0,8},{8,16},{16,24},{24,32},{32,40},{40,48},{48,56},{56,64},{64,7... | collective-permute-start | bytes 57608 | tf_op jit(solution)/shard_map/ppermute | solution.py:29
  23.1 52.0 %copy-start.29 = (s32[3072,1]{0,1:T(1,128)}, s32[3072,1]{0,1:T(1,128)S(1)}, u32[]{:S(2)}) copy-start(s32[3072,1]{0,1:T(1,128)S(1)} %compare_select_fusion.3) | copy-start | bytes 36868
  24.8 50.3 %copy-start.11 = (s32[4,2048]{1,0:T(4,128)S(1)}, s32[4,2048]{1,0:T(4,128)}, u32[]{:S(2)}) copy-start(s32[4,2048]{1,0:T(4,128)} %param.11) | copy-start | bytes 98308
  24.8 50.4 %copy-start.9 = (f32[150,2048]{1,0:T(8,128)S(1)}, f32[150,2048]{1,0:T(8,128)}, u32[]{:S(2)}) copy-start(f32[150,2048]{1,0:T(8,128)} %param.13) | copy-start | bytes 3686404
  26.1 13.7 %collective-permute-start = (f32[5,30,128]{2,1,0:T(8,128)S(1)}, f32[5,30,128]{2,1,0:T(8,128)S(1)}, u32[]{:S(2)}, u32[]{:S(2)}) collective-permute-start(f32[5,30,128]{2,1,0:T(8,128)S(1)} %reshape_squeeze.36), channel_id=1, source_target_pairs={{0,1},{1,2},{2,3},{3,4},{4,5},{5,6},{6,7},{8,9},{9,10},{10,11},{11... | collective-permute-start | bytes 230408 | tf_op jit(solution)/shard_map/ppermute | solution.py:20
  28.6 11.2 %collective-permute-start.1 = (f32[5,30,128]{2,1,0:T(8,128)S(1)}, f32[5,30,128]{2,1,0:T(8,128)S(1)}, u32[]{:S(2)}, u32[]{:S(2)}) collective-permute-start(f32[5,30,128]{2,1,0:T(8,128)S(1)} %reshape_squeeze.37), channel_id=1, source_target_pairs={{1,0},{2,1},{3,2},{4,3},{5,4},{6,5},{7,6},{9,8},{10,9},{11,10},{12... | collective-permute-start | bytes 230408 | tf_op jit(solution)/shard_map/ppermute | solution.py:20
  32.9 6.9 %collective-permute-start.3 = (f32[5,30,32]{2,1,0:T(8,128)S(1)}, f32[5,30,32]{2,1,0:T(8,128)S(1)}, u32[]{:S(2)}, u32[]{:S(2)}) collective-permute-start(f32[5,30,32]{2,1,0:T(8,128)S(1)} %reshape_squeeze.39), channel_id=1, source_target_pairs={{8,0},{16,8},{24,16},{32,24},{40,32},{48,40},{56,48},{64,56},{72,6... | collective-permute-start | bytes 57608 | tf_op jit(solution)/shard_map/ppermute | solution.py:29
  62.6 14.4 %collective-permute-start.10 = (f32[5,30,32]{2,1,0:T(8,128)}, f32[5,30,32]{2,1,0:T(8,128)S(1)}, u32[]{:S(2)}, u32[]{:S(2)}) collective-permute-start(f32[5,30,32]{2,1,0:T(8,128)} %get-tuple-element.17), channel_id=1, source_target_pairs={{0,8},{8,16},{16,24},{24,32},{32,40},{40,48},{48,56},{56,64},{64,7... | collective-permute-start | bytes 57608 | tf_op jit(solution)/shard_map/ppermute | solution.py:29
  62.7 14.4 %collective-permute-start.11 = (f32[5,30,32]{2,1,0:T(8,128)}, f32[5,30,32]{2,1,0:T(8,128)S(1)}, u32[]{:S(2)}, u32[]{:S(2)}) collective-permute-start(f32[5,30,32]{2,1,0:T(8,128)} %get-tuple-element.18), channel_id=1, source_target_pairs={{8,0},{16,8},{24,16},{32,24},{40,32},{48,40},{56,48},{64,56},{72,6... | collective-permute-start | bytes 57608 | tf_op jit(solution)/shard_map/ppermute | solution.py:29
  68.2 8.9 %collective-permute-start.8 = (f32[5,30,128]{2,1,0:T(8,128)}, f32[5,30,128]{2,1,0:T(8,128)S(1)}, u32[]{:S(2)}, u32[]{:S(2)}) collective-permute-start(f32[5,30,128]{2,1,0:T(8,128)} %get-tuple-element.15), channel_id=1, source_target_pairs={{0,1},{1,2},{2,3},{3,4},{4,5},{5,6},{6,7},{8,9},{9,10},{10,11},{11... | collective-permute-start | bytes 230408 | tf_op jit(solution)/shard_map/ppermute | solution.py:20
  70.1 7.6 %collective-permute-start.9 = (f32[5,30,128]{2,1,0:T(8,128)}, f32[5,30,128]{2,1,0:T(8,128)S(1)}, u32[]{:S(2)}, u32[]{:S(2)}) collective-permute-start(f32[5,30,128]{2,1,0:T(8,128)} %get-tuple-element.16), channel_id=1, source_target_pairs={{1,0},{2,1},{3,2},{4,3},{5,4},{6,5},{7,6},{9,8},{10,9},{11,10},{12... | collective-permute-start | bytes 230408 | tf_op jit(solution)/shard_map/ppermute | solution.py:20
  124.7 49.1 %all-to-all-start = ((f32[150,128,24]{0,2,1:T(8,128)}), f32[150,128,24]{0,2,1:T(8,128)S(1)}, u32[]{:S(2)}, u32[]{:S(2)}) async-start(f32[150,128,24]{0,2,1:T(8,128)} %broadcast_select_fusion), calls=%async_computation | async-start | bytes 6291456 | tf_op jit(solution)/shard_map/all_to_all | solution.py:132
  334.8 22.3 %collective-permute-start.12 = (f32[5,30,128]{2,1,0:T(8,128)S(1)}, f32[5,30,128]{2,1,0:T(8,128)S(1)}, u32[]{:S(2)}, u32[]{:S(2)}) collective-permute-start(f32[5,30,128]{2,1,0:T(8,128)S(1)} %reshape_squeeze.44), channel_id=1, source_target_pairs={{0,1},{1,2},{2,3},{3,4},{4,5},{5,6},{6,7},{8,9},{9,10},{10,11},{11... | collective-permute-start | bytes 230408 | tf_op jit(solution)/shard_map/ppermute | solution.py:20
  337.5 19.6 %collective-permute-start.13 = (f32[5,30,128]{2,1,0:T(8,128)S(1)}, f32[5,30,128]{2,1,0:T(8,128)S(1)}, u32[]{:S(2)}, u32[]{:S(2)}) collective-permute-start(f32[5,30,128]{2,1,0:T(8,128)S(1)} %reshape_squeeze.45), channel_id=1, source_target_pairs={{1,0},{2,1},{3,2},{4,3},{5,4},{6,5},{7,6},{9,8},{10,9},{11,10},{12... | collective-permute-start | bytes 230408 | tf_op jit(solution)/shard_map/ppermute | solution.py:20
  342.8 14.2 %collective-permute-start.14 = (f32[5,30,32]{2,1,0:T(8,128)S(1)}, f32[5,30,32]{2,1,0:T(8,128)S(1)}, u32[]{:S(2)}, u32[]{:S(2)}) collective-permute-start(f32[5,30,32]{2,1,0:T(8,128)S(1)} %reshape_squeeze.46), channel_id=1, source_target_pairs={{0,8},{8,16},{16,24},{24,32},{32,40},{40,48},{48,56},{56,64},{64,7... | collective-permute-start | bytes 57608 | tf_op jit(solution)/shard_map/ppermute | solution.py:29
  343.0 14.0 %collective-permute-start.15 = (f32[5,30,32]{2,1,0:T(8,128)S(1)}, f32[5,30,32]{2,1,0:T(8,128)S(1)}, u32[]{:S(2)}, u32[]{:S(2)}) collective-permute-start(f32[5,30,32]{2,1,0:T(8,128)S(1)} %reshape_squeeze.47), channel_id=1, source_target_pairs={{8,0},{16,8},{24,16},{32,24},{40,32},{48,40},{56,48},{64,56},{72,6... | collective-permute-start | bytes 57608 | tf_op jit(solution)/shard_map/ppermute | solution.py:29
  380.4 14.6 %collective-permute-start.16 = (f32[5,30,128]{2,1,0:T(8,128)}, f32[5,30,128]{2,1,0:T(8,128)S(1)}, u32[]{:S(2)}, u32[]{:S(2)}) collective-permute-start(f32[5,30,128]{2,1,0:T(8,128)} %get-tuple-element.21), channel_id=1, source_target_pairs={{0,1},{1,2},{2,3},{3,4},{4,5},{5,6},{6,7},{8,9},{9,10},{10,11},{11... | collective-permute-start | bytes 230408 | tf_op jit(solution)/shard_map/ppermute | solution.py:20
  382.4 12.6 %collective-permute-start.17 = (f32[5,30,128]{2,1,0:T(8,128)}, f32[5,30,128]{2,1,0:T(8,128)S(1)}, u32[]{:S(2)}, u32[]{:S(2)}) collective-permute-start(f32[5,30,128]{2,1,0:T(8,128)} %get-tuple-element.22), channel_id=1, source_target_pairs={{1,0},{2,1},{3,2},{4,3},{5,4},{6,5},{7,6},{9,8},{10,9},{11,10},{12... | collective-permute-start | bytes 230408 | tf_op jit(solution)/shard_map/ppermute | solution.py:20
  387.2 7.8 %collective-permute-start.18 = (f32[5,30,32]{2,1,0:T(8,128)}, f32[5,30,32]{2,1,0:T(8,128)S(1)}, u32[]{:S(2)}, u32[]{:S(2)}) collective-permute-start(f32[5,30,32]{2,1,0:T(8,128)} %get-tuple-element.23), channel_id=1, source_target_pairs={{0,8},{8,16},{16,24},{24,32},{32,40},{40,48},{48,56},{56,64},{64,7... | collective-permute-start | bytes 57608 | tf_op jit(solution)/shard_map/ppermute | solution.py:29
  387.3 7.7 %collective-permute-start.19 = (f32[5,30,32]{2,1,0:T(8,128)}, f32[5,30,32]{2,1,0:T(8,128)S(1)}, u32[]{:S(2)}, u32[]{:S(2)}) collective-permute-start(f32[5,30,32]{2,1,0:T(8,128)} %get-tuple-element.24), channel_id=1, source_target_pairs={{8,0},{16,8},{24,16},{32,24},{40,32},{48,40},{56,48},{64,56},{72,6... | collective-permute-start | bytes 57608 | tf_op jit(solution)/shard_map/ppermute | solution.py:29
  (27 other events, 144.9 us)
